TPU v7x, 512 devices: a whole 4x8x8 slice. The times are simulated.
512 devices in a mesh: grp: 8 (over x, core), blk: 64 (over y, z).
Axes of the slice: x: 4, y: 8, z: 8, core: 2. Of those that a mesh axis runs over, the one named last changes fastest.
Arguments:
- features: bfloat16 [65536, 256], P(('grp', 'blk')), may hold values from -6 to 6
- dest: int32 [65536, 1], P(('grp', 'blk')), may hold values from 0 to 63; in each aligned block of 128 rows (0 to 127, 128 to 255, ...) at most 4 rows name the same one
- placement: int32 [512, 256], P(('grp', 'blk')), may hold values from 0 to 255, each once within a row
- weight: bfloat16 [27, 256, 128], replicated, may hold values from -0.078125 to 0.078125
- grad_out: bfloat16 [64, 512, 4, 128], P('grp', 'blk'), may hold values from -6 to 6
Outputs:
- output: bfloat16 [64, 512, 4, 128], P('grp', 'blk')
- grad_rows: bfloat16 [65536, 256], P(('grp', 'blk'))
- weight_grad: bfloat16 [27, 256, 128], replicated
Inputs may be any that keep to these rules, and one draw needn't show every extreme that they name: `dest`: among the rows of one device no value is named by more than 4 rows, a bound that some block reaches. `placement`: each row is a permutation of 0 to 255.
All inputs are finite; a program needn't handle non-finite values.
Results may differ from a plain program's by a relative error of at most 0.0013.
Values may be sent and summed in bfloat16 or wider, within the bound.
A program may use at most 64 MiB of HBM per device.

v0:
```python
import math
import jax
import jax.numpy as jnp
from jax import lax
from jax.sharding import PartitionSpec as P


def extended(cells, sides, width):
    for axis, dim in sides:
        count = lax.axis_size(axis)
        ends = count - 1
        head = lax.slice_in_dim(cells, 0, width, axis=dim)
        tail = lax.slice_in_dim(cells, cells.shape[dim] - width, cells.shape[dim], axis=dim)
        cells = jnp.concatenate(
            [
                lax.ppermute(tail, axis, [(i, (i + 1) % count) for i in range(ends)]),
                cells,
                lax.ppermute(head, axis, [((i + 1) % count, i) for i in range(ends)]),
            ],
            axis=dim,
        )
    return cells


def shards(features, dest, placement, weight, grad_out):
    row_count, channels = features.shape
    blk_count = lax.axis_size("blk")
    grp_count = lax.axis_size("grp")
    voxel_of_slot = placement[0]
    voxel_count = voxel_of_slot.shape[0]
    capacity = voxel_count // blk_count
    size_x, size_y, size_z, out_channels = grad_out.shape
    target = dest[:, 0]
    owners = jnp.arange(blk_count, dtype=jnp.int32)
    one_hot = (target[:, None] == owners[None, :]).astype(jnp.int32)
    slot_rank = jnp.sum((jnp.cumsum(one_hot, axis=0) - one_hot) * one_hot, axis=1)
    send_counts = jnp.sum(one_hot, axis=0).reshape(blk_count, 1)
    slot_index = target * capacity + slot_rank
    outgoing = jnp.zeros((voxel_count, channels), jnp.bfloat16).at[slot_index].set(features)
    incoming, recv_counts = (
        lax.all_to_all(
            outgoing.reshape(blk_count, capacity, channels),
            "blk",
            split_axis=0,
            concat_axis=0,
            tiled=True,
        ),
        lax.all_to_all(send_counts, "blk", split_axis=0, concat_axis=0, tiled=True),
    )
    filled = (
        (jnp.arange(capacity, dtype=jnp.int32)[None, :] < recv_counts)
        .reshape(-1)
        .astype(jnp.float32)
    )
    voxel_rows = (
        jnp.zeros((voxel_count, channels), jnp.bfloat16)
        .at[voxel_of_slot]
        .set(incoming.reshape(voxel_count, channels))
    )
    occupied = jnp.zeros((voxel_count,), jnp.float32).at[voxel_of_slot].set(filled)[:, None]
    voxel_grid = voxel_rows.reshape(size_x, size_y, size_z, channels)
    padded = extended(voxel_grid, (("grp", 0), ("blk", 1)), 1)
    padded = jnp.pad(padded, ((0, 0), (0, 0), (1, 1), (0, 0)))
    shifted = []
    total = jnp.zeros((voxel_count, out_channels), jnp.float32)
    for offset in range(27):
        shift_x, shift_y, shift_z = (offset // 9, offset // 3 % 3, offset % 3)
        window = padded[
            shift_x : shift_x + size_x, shift_y : shift_y + size_y, shift_z : shift_z + size_z
        ].reshape(voxel_count, channels)
        shifted.append(window)
        total = total + jnp.dot(window, weight[offset], preferred_element_type=jnp.float32)
    output = (total * occupied).astype(jnp.bfloat16).reshape(size_x, size_y, size_z, out_channels)
    masked_grad = (
        grad_out.reshape(voxel_count, out_channels).astype(jnp.float32) * occupied
    ).astype(jnp.bfloat16)
    grad_padded = extended(
        masked_grad.reshape(size_x, size_y, size_z, out_channels), (("grp", 0), ("blk", 1)), 1
    )
    grad_padded = jnp.pad(grad_padded, ((0, 0), (0, 0), (1, 1), (0, 0)))
    back_total = jnp.zeros((voxel_count, channels), jnp.float32)
    partials = []
    for offset in range(27):
        shift_x, shift_y, shift_z = (offset // 9, offset // 3 % 3, offset % 3)
        window = grad_padded[
            2 - shift_x : 2 - shift_x + size_x,
            2 - shift_y : 2 - shift_y + size_y,
            2 - shift_z : 2 - shift_z + size_z,
        ].reshape(voxel_count, out_channels)
        back_total = back_total + lax.dot_general(
            window, weight[offset], (((1,), (1,)), ((), ())), preferred_element_type=jnp.float32
        )
        partials.append(
            lax.dot_general(
                shifted[offset],
                masked_grad,
                (((0,), (0,)), ((), ())),
                preferred_element_type=jnp.float32,
            )
        )
    grad_grid = (back_total * occupied).astype(jnp.bfloat16)
    weight_terms = jnp.stack(partials).reshape(27 * channels, out_channels)
    grad_scale = 1.0 / math.sqrt(row_count * blk_count * grp_count)
    weight_grad = (lax.psum(weight_terms, ("grp", "blk")) * grad_scale).astype(jnp.bfloat16)
    weight_grad = weight_grad.reshape(27, channels, out_channels)
    returning = grad_grid[voxel_of_slot].reshape(blk_count, capacity, channels)
    returned = lax.all_to_all(returning, "blk", split_axis=0, concat_axis=0, tiled=True)
    grad_rows = returned.reshape(voxel_count, channels)[slot_index]
    return (output, grad_rows, weight_grad)


def solution(mesh):
    in_specs = (
        P(("grp", "blk"), None),
        P(("grp", "blk"), None),
        P(("grp", "blk"), None),
        P(),
        P("grp", "blk", None, None),
    )
    out_specs = (P("grp", "blk", None, None), P(("grp", "blk"), None), P())
    return jax.shard_map(shards, mesh=mesh, in_specs=in_specs, out_specs=out_specs, check_vma=False)
```

profile of v0, /device:TPU:24, one launch (start us, length us, event | category | flops | bytes accessed | tf_op | source)
XLA Modules:
  0.0 480.3 jit_solution(8768574311076272875)
XLA Ops:
  9.6 16.4 %all-to-all-start.1 = ((s32[64,1,1]{2,1,0:T(1,128)}), s32[64,1,1]{2,1,0:T(1,128)S(1)}, u32[]{:S(2)}, u32[]{:S(2)}) async-start(s32[64,1,1]{2,1,0:T(1,128)} %copy.183), calls=%async_computation.1 | async-start | bytes 65536 | tf_op jit(solution)/shard_map/all_to_all | solution.py:48
  29.5 5.8 %all-to-all-done.1 = s32[64,1,1]{2,1,0:T(1,128)S(1)} async-done(((s32[64,1,1]{2,1,0:T(1,128)}), s32[64,1,1]{2,1,0:T(1,128)S(1)}, u32[]{:S(2)}, u32[]{:S(2)}) %all-to-all-start.1) | async-done | bytes 288 | tf_op jit(solution)/shard_map/all_to_all | solution.py:48
  35.3 7.3 %all-to-all-start = ((bf16[64,4,256]{2,1,0:T(4,128)(2,1)}), bf16[64,4,256]{2,1,0:T(4,128)(2,1)S(1)}, u32[]{:S(2)}, u32[]{:S(2)}) async-start(bf16[64,4,256]{2,1,0:T(4,128)(2,1)} %reshape.379), calls=%async_computation | async-start | bytes 262144 | tf_op jit(solution)/shard_map/all_to_all | solution.py:41
  47.8 3.0 collective-permute-start.4
  51.8 3.4 collective-permute-start.6
  55.2 4.6 collective-permute-start.7
  68.6 1.9 collective-permute-start
  72.5 12.3 %all-to-all-start.2 = ((bf16[64,4,256]{2,1,0:T(4,128)(2,1)}), bf16[64,4,256]{2,1,0:T(4,128)(2,1)S(1)}, u32[]{:S(2)}, u32[]{:S(2)}) async-start(bf16[64,4,256]{2,1,0:T(4,128)(2,1)} %reshape.436), calls=%async_computation.2 | async-start | bytes 262144 | tf_op jit(solution)/shard_map/all_to_all | solution.py:107
  86.4 4.1 collective-permute-done.1
  90.6 3.4 collective-permute-start.2
  93.9 4.8 collective-permute-start.3
  119.0 1.6 copy.176
  122.2 1.6 copy.175
  125.4 1.6 copy.173
  128.6 1.6 copy.172
  131.8 1.6 copy.170
  133.4 1.6 reshape.396
  135.0 1.6 copy.169
  138.2 1.6 copy.168
  141.4 1.6 copy.167
  143.0 1.6 reshape.393
  144.6 1.6 copy.165
  147.8 1.6 copy.164
  151.0 1.6 copy.162
  154.9 1.6 reshape.387
  156.5 1.6 copy.158
  159.7 1.6 copy.157
  161.3 1.6 reshape.384
  163.0 1.6 copy.155
  182.7 1.8 copy-done.2
  188.6 281.5 %all-reduce.4.cloned.1.call-done = f32[6912,128]{1,0:T(8,128)} async-done(((f32[6912,128]{1,0:T(8,128)}), f32[6912,128]{1,0:T(8,128)}) %all-reduce.4.cloned.1.call-update) | async-done | bytes 3538960 | tf_op jit(solution)/shard_map/psum | solution.py:104
  470.1 3.4 multiply_convert_fusion
  (238 shorter events, 82.6 us)
Async XLA Ops:
  9.6 25.6 %all-to-all-start.1 = ((s32[64,1,1]{2,1,0:T(1,128)}), s32[64,1,1]{2,1,0:T(1,128)S(1)}, u32[]{:S(2)}, u32[]{:S(2)}) async-start(s32[64,1,1]{2,1,0:T(1,128)} %copy.183), calls=%async_computation.1 | async-start | bytes 65536 | tf_op jit(solution)/shard_map/all_to_all | solution.py:48
  35.3 31.7 %all-to-all-start = ((bf16[64,4,256]{2,1,0:T(4,128)(2,1)}), bf16[64,4,256]{2,1,0:T(4,128)(2,1)S(1)}, u32[]{:S(2)}, u32[]{:S(2)}) async-start(bf16[64,4,256]{2,1,0:T(4,128)(2,1)} %reshape.379), calls=%async_computation | async-start | bytes 262144 | tf_op jit(solution)/shard_map/all_to_all | solution.py:41
  42.6 19.2 %copy-start = (bf16[27,256,128]{2,1,0:T(8,128)(2,1)S(1)}, bf16[27,256,128]{2,1,0:T(8,128)(2,1)}, u32[]{:S(2)}) copy-start(bf16[27,256,128]{2,1,0:T(8,128)(2,1)} %param.8) | copy-start | bytes 5308420
  46.5 5.3 %collective-permute-start.5 = (bf16[1,8,4,128]{3,2,1,0:T(4,128)(2,1)S(1)}, bf16[1,8,4,128]{3,2,1,0:T(4,128)(2,1)S(1)}, u32[]{:S(2)}, u32[]{:S(2)}) collective-permute-start(bf16[1,8,4,128]{3,2,1,0:T(4,128)(2,1)S(1)} %bitcast.495), channel_id=1, source_target_pairs={{64,0},{128,64},{192,128},{256,192},{320,256},{384,320},{448,384},... | collective-permute-start | bytes 24584 | tf_op jit(solution)/shard_map/ppermute | solution.py:18
  47.8 4.0 collective-permute-start.4
  51.8 8.0 %collective-permute-start.6 = (bf16[10,1,4,128]{3,2,1,0:T(4,128)(2,1)S(1)}, bf16[10,1,4,128]{3,2,1,0:T(4,128)(2,1)S(1)}, u32[]{:S(2)}, u32[]{:S(2)}) collective-permute-start(bf16[10,1,4,128]{3,2,1,0:T(4,128)(2,1)S(1)} %get-tuple-element.65), channel_id=1, source_target_pairs={{0,1},{1,2},{2,3},{3,4},{4,5},{5,6},{6,7},{7,8},{8,9},{9,10},{10,1... | collective-permute-start | bytes 30728 | tf_op jit(solution)/shard_map/ppermute | solution.py:16
  55.2 5.9 %collective-permute-start.7 = (bf16[10,1,4,128]{3,2,1,0:T(4,128)(2,1)S(1)}, bf16[10,1,4,128]{3,2,1,0:T(4,128)(2,1)S(1)}, u32[]{:S(2)}, u32[]{:S(2)}) collective-permute-start(bf16[10,1,4,128]{3,2,1,0:T(4,128)(2,1)S(1)} %get-tuple-element.66), channel_id=1, source_target_pairs={{1,0},{2,1},{3,2},{4,3},{5,4},{6,5},{7,6},{8,7},{9,8},{10,9},{11,1... | collective-permute-start | bytes 30728 | tf_op jit(solution)/shard_map/ppermute | solution.py:18
  68.6 17.7 %collective-permute-start = (bf16[1,8,4,256]{3,1,2,0:T(8,128)(2,1)S(1)}, bf16[1,8,4,256]{3,1,2,0:T(8,128)(2,1)S(1)}, u32[]{:S(2)}, u32[]{:S(2)}) collective-permute-start(bf16[1,8,4,256]{3,1,2,0:T(8,128)(2,1)S(1)} %copy.152), channel_id=1, source_target_pairs={{0,64},{64,128},{128,192},{192,256},{256,320},{320,384},{384,448},... | collective-permute-start | bytes 49160 | tf_op jit(solution)/shard_map/ppermute | solution.py:16
  72.5 27.1 %all-to-all-start.2 = ((bf16[64,4,256]{2,1,0:T(4,128)(2,1)}), bf16[64,4,256]{2,1,0:T(4,128)(2,1)S(1)}, u32[]{:S(2)}, u32[]{:S(2)}) async-start(bf16[64,4,256]{2,1,0:T(4,128)(2,1)} %reshape.436), calls=%async_computation.2 | async-start | bytes 262144 | tf_op jit(solution)/shard_map/all_to_all | solution.py:107
  84.9 385.2 %all-reduce.4.cloned.1.call-start = ((), (), s32[]{:S(2)}) async-start(), calls=%async_computation.3 | async-start | bytes 7077888 | tf_op jit(solution)/shard_map/psum | solution.py:104
  85.0 13.8 %copy-start.18 = (bf16[8,8,4,256]{3,2,1,0:T(4,128)(2,1)}, bf16[8,8,4,256]{3,2,1,0:T(4,128)(2,1)S(1)}, u32[]{:S(2)}) copy-start(bf16[8,8,4,256]{3,2,1,0:T(4,128)(2,1)S(1)} %reshape.381) | copy-start | bytes 393220
  85.0 5.5 %collective-permute-start.1 = (bf16[1,8,4,256]{3,1,2,0:T(8,128)(2,1)S(1)}, bf16[1,8,4,256]{3,1,2,0:T(8,128)(2,1)S(1)}, u32[]{:S(2)}, u32[]{:S(2)}) collective-permute-start(bf16[1,8,4,256]{3,1,2,0:T(8,128)(2,1)S(1)} %copy.153), channel_id=1, source_target_pairs={{64,0},{128,64},{192,128},{256,192},{320,256},{384,320},{448,384},... | collective-permute-start | bytes 49160 | tf_op jit(solution)/shard_map/ppermute | solution.py:18
  86.4 14.8 %copy-start.31 = (bf16[9,8,4,256]{3,1,2,0:T(8,128)(2,1)}, bf16[9,8,4,256]{3,1,2,0:T(8,128)(2,1)S(1)}, u32[]{:S(2)}) copy-start(bf16[9,8,4,256]{3,1,2,0:T(8,128)(2,1)S(1)} %get-tuple-element.53) | copy-start | bytes 442372
  90.5 8.3 %copy-start.27 = (bf16[9,8,4,256]{3,1,2,0:T(8,128)(2,1)}, bf16[9,8,4,256]{3,1,2,0:T(8,128)(2,1)S(1)}, u32[]{:S(2)}) copy-start(bf16[9,8,4,256]{3,1,2,0:T(8,128)(2,1)S(1)} %get-tuple-element.71) | copy-start | bytes 442372
  90.6 10.6 %collective-permute-start.2 = (bf16[10,1,4,256]{3,1,2,0:T(2,128)(2,1)S(1)}, bf16[10,1,4,256]{3,1,2,0:T(2,128)(2,1)S(1)}, u32[]{:S(2)}, u32[]{:S(2)}) collective-permute-start(bf16[10,1,4,256]{3,1,2,0:T(2,128)(2,1)S(1)} %get-tuple-element.50), channel_id=1, source_target_pairs={{0,1},{1,2},{2,3},{3,4},{4,5},{5,6},{6,7},{7,8},{8,9},{9,10},{10,1... | collective-permute-start | bytes 61448 | tf_op jit(solution)/shard_map/ppermute | solution.py:16
  93.9 7.2 %collective-permute-start.3 = (bf16[10,1,4,256]{3,1,2,0:T(2,128)(2,1)S(1)}, bf16[10,1,4,256]{3,1,2,0:T(2,128)(2,1)S(1)}, u32[]{:S(2)}, u32[]{:S(2)}) collective-permute-start(bf16[10,1,4,256]{3,1,2,0:T(2,128)(2,1)S(1)} %get-tuple-element.51), channel_id=1, source_target_pairs={{1,0},{2,1},{3,2},{4,3},{5,4},{6,5},{7,6},{8,7},{9,8},{10,9},{11,1... | collective-permute-start | bytes 61448 | tf_op jit(solution)/shard_map/ppermute | solution.py:18
  105.5 1.8 copy-start.20
  154.9 15.8 %copy-start.8 = (bf16[256,256]{1,0:T(8,128)(2,1)S(1)}, bf16[256,256]{1,0:T(8,128)(2,1)}, u32[]{:S(2)}) copy-start(bf16[256,256]{1,0:T(8,128)(2,1)} %reshape.386) | copy-start | bytes 393220
  166.2 4.7 copy-start.17
  166.2 4.9 %copy-start.16 = (bf16[256,256]{1,0:T(8,128)(2,1)S(1)}, bf16[256,256]{1,0:T(8,128)(2,1)}, u32[]{:S(2)}) copy-start(bf16[256,256]{1,0:T(8,128)(2,1)} %reshape.388) | copy-start | bytes 393220
  166.2 5.1 %copy-start.11 = (bf16[256,256]{1,0:T(8,128)(2,1)S(1)}, bf16[256,256]{1,0:T(8,128)(2,1)}, u32[]{:S(2)}) copy-start(bf16[256,256]{1,0:T(8,128)(2,1)} %reshape.389) | copy-start | bytes 393220
  166.2 5.3 %copy-start.15 = (bf16[256,256]{1,0:T(8,128)(2,1)S(1)}, bf16[256,256]{1,0:T(8,128)(2,1)}, u32[]{:S(2)}) copy-start(bf16[256,256]{1,0:T(8,128)(2,1)} %reshape.390) | copy-start | bytes 393220
  167.3 4.3 copy-start.14
  168.4 3.4 copy-start.10
  169.5 2.5 copy-start.13
  170.7 1.5 copy-start.12
  170.9 1.7 copy-start.26
  171.1 2.0 copy-start.1
  182.7 1.8 copy-start.2
  184.5 1.4 copy-start.6
  185.4 1.3 copy-start.4
  185.4 1.5 copy-start.3
  (13 other events, 11.8 us)
Sparse Core Ops, SparseCore 0:
  184.6 285.4 all-reduce.3
where the time goes:
time: 482 us; the launch traced here: 480 us
  waiting for transfers between devices  293 us (61%)
  local copies, waits for them, and re-layouts  80.7 us (17%)
  starting transfers between devices  59.6 us (12%)
  matrix products  20.7 us (4%)
  between operations  15.2 us (3%)
  other arithmetic  11.4 us (2%)
    psum x1, waiting for transfers between devices, shards(): lax.psum(weight_terms, ('grp', 'blk')) * grad_scale  282 us
    slice x29, local copies, waits for them, and re-layouts, shards(): padded[shift_x:shift_x + size_x, shift_y:shift_y + size_y, shift_z:shift_...  32.4 us
    reshape x26, local copies, waits for them, and re-layouts, shards(): window = padded[shift_x:shift_x + size_x, shift_y:shift_y + size_y, shift...  30.6 us
    all_to_all x1, starting transfers between devices, shards(): lax.all_to_all(send_counts, 'blk', split_axis=0, concat_axis=0, tiled=True)  16.4 us
    all_to_all x1, starting transfers between devices, shards(): lax.all_to_all(returning, 'blk', split_axis=0, concat_axis=0, tiled=True)  12.3 us
    ppermute x4, starting transfers between devices, extended(): lax.ppermute(head, axis, [((i + 1) % count, i) for i in range(ends)])  11.9 us
    ppermute x4, starting transfers between devices, extended(): lax.ppermute(tail, axis, [(i, (i + 1) % count) for i in range(ends)])  11.7 us
  transfers between devices with their start and end apart: 12, of which 4 were waited for; matrix products, arithmetic and copies ran while one was open for 4% of the time, Pallas kernels for 0%

commit v1 on v0

--- a/solution.py
+++ b/solution.py
@@ -101,7 +101,8 @@
     grad_grid = (back_total * occupied).astype(jnp.bfloat16)
     weight_terms = jnp.stack(partials).reshape(27 * channels, out_channels)
     grad_scale = 1.0 / math.sqrt(row_count * blk_count * grp_count)
-    weight_grad = (lax.psum(weight_terms, ("grp", "blk")) * grad_scale).astype(jnp.bfloat16)
+    form_seats_all_by_axis = lambda mine: lax.psum(lax.psum(mine, "blk"), "grp")
+    weight_grad = (form_seats_all_by_axis(weight_terms) * grad_scale).astype(jnp.bfloat16)
     weight_grad = weight_grad.reshape(27, channels, out_channels)
     returning = grad_grid[voxel_of_slot].reshape(blk_count, capacity, channels)
     returned = lax.all_to_all(returning, "blk", split_axis=0, concat_axis=0, tiled=True)

time: 482 us -> 402 us (0.83)
  the two profiles are of different devices: /device:TPU:24 before, /device:TPU:8 now
where the time goes in v1:
time: 402 us; the launch traced here: 401 us
  waiting for transfers between devices  209 us (52%)
  local copies, waits for them, and re-layouts  69.7 us (17%)
  starting transfers between devices  58.1 us (14%)
  matrix products  38.3 us (10%)
  between operations  15.1 us (4%)
  other arithmetic  11.3 us (3%)
    psum x2, waiting for transfers between devices, shards(): form_seats_all_by_axis = lambda mine: lax.psum(lax.psum(mine, 'blk'), 'grp')  196 us
    reshape x26, local copies, waits for them, and re-layouts, shards(): window = padded[shift_x:shift_x + size_x, shift_y:shift_y + size_y, shift...  31.9 us
    dot_general x27, matrix products, shards(): lax.dot_general(shifted[offset], masked_grad, (((0,), (0,)), ((), ())), p...  24.7 us
    slice x29, local copies, waits for them, and re-layouts, shards(): padded[shift_x:shift_x + size_x, shift_y:shift_y + size_y, shift_z:shift_...  23.9 us
    all_to_all x1, starting transfers between devices, shards(): lax.all_to_all(send_counts, 'blk', split_axis=0, concat_axis=0, tiled=True)  16.6 us
    all_to_all x1, starting transfers between devices, shards(): lax.all_to_all(returning, 'blk', split_axis=0, concat_axis=0, tiled=True)  12.4 us
    ppermute x4, starting transfers between devices, extended(): lax.ppermute(head, axis, [((i + 1) % count, i) for i in range(ends)])  11.9 us
    ppermute x4, starting transfers between devices, extended(): lax.ppermute(tail, axis, [(i, (i + 1) % count) for i in range(ends)])  11.7 us
  transfers between devices with their start and end apart: 13, of which 5 were waited for; matrix products, arithmetic and copies ran while one was open for 17% of the time, Pallas kernels for 0%

profile of v1, /device:TPU:8, one launch (start us, length us, event | category | flops | bytes accessed | tf_op | source)
XLA Modules:
  0.0 401.1 jit_solution(11206996014002651126)
XLA Ops:
  9.6 16.6 %all-to-all-start.1 = ((s32[64,1,1]{2,1,0:T(1,128)}), s32[64,1,1]{2,1,0:T(1,128)S(1)}, u32[]{:S(2)}, u32[]{:S(2)}) async-start(s32[64,1,1]{2,1,0:T(1,128)} %copy.183), calls=%async_computation.1 | async-start | bytes 65536 | tf_op jit(solution)/shard_map/all_to_all | solution.py:48
  29.7 7.5 %all-to-all-done.1 = s32[64,1,1]{2,1,0:T(1,128)S(1)} async-done(((s32[64,1,1]{2,1,0:T(1,128)}), s32[64,1,1]{2,1,0:T(1,128)S(1)}, u32[]{:S(2)}, u32[]{:S(2)}) %all-to-all-start.1) | async-done | bytes 288 | tf_op jit(solution)/shard_map/all_to_all | solution.py:48
  37.2 5.5 %all-to-all-start = ((bf16[64,4,256]{2,1,0:T(4,128)(2,1)}), bf16[64,4,256]{2,1,0:T(4,128)(2,1)S(1)}, u32[]{:S(2)}, u32[]{:S(2)}) async-start(bf16[64,4,256]{2,1,0:T(4,128)(2,1)} %reshape.379), calls=%async_computation | async-start | bytes 262144 | tf_op jit(solution)/shard_map/all_to_all | solution.py:41
  47.9 3.0 collective-permute-start.4
  51.9 3.4 collective-permute-start.6
  55.3 4.6 %collective-permute-start.7 = (bf16[10,1,4,128]{3,2,1,0:T(4,128)(2,1)S(1)}, bf16[10,1,4,128]{3,2,1,0:T(4,128)(2,1)S(1)}, u32[]{:S(2)}, u32[]{:S(2)}) collective-permute-start(bf16[10,1,4,128]{3,2,1,0:T(4,128)(2,1)S(1)} %get-tuple-element.66), channel_id=1, source_target_pairs={{1,0},{2,1},{3,2},{4,3},{5,4},{6,5},{7,6},{8,7},{9,8},{10,9},{11,1... | collective-permute-start | bytes 30728 | tf_op jit(solution)/shard_map/ppermute | solution.py:18
  68.7 1.9 collective-permute-start
  72.6 12.4 %all-to-all-start.2 = ((bf16[64,4,256]{2,1,0:T(4,128)(2,1)}), bf16[64,4,256]{2,1,0:T(4,128)(2,1)S(1)}, u32[]{:S(2)}, u32[]{:S(2)}) async-start(bf16[64,4,256]{2,1,0:T(4,128)(2,1)} %reshape.436), calls=%async_computation.2 | async-start | bytes 262144 | tf_op jit(solution)/shard_map/all_to_all | solution.py:108
  86.6 4.1 %collective-permute-done.1 = bf16[1,8,4,256]{3,1,2,0:T(8,128)(2,1)S(1)} collective-permute-done((bf16[1,8,4,256]{3,1,2,0:T(8,128)(2,1)S(1)}, bf16[1,8,4,256]{3,1,2,0:T(8,128)(2,1)S(1)}, u32[]{:S(2)}, u32[]{:S(2)}) %collective-permute-start.1) | collective-permute-done | bytes 16416 | tf_op jit(solution)/shard_map/ppermute | solution.py:18
  90.7 3.4 collective-permute-start.2
  94.1 4.8 %collective-permute-start.3 = (bf16[10,1,4,256]{3,1,2,0:T(2,128)(2,1)S(1)}, bf16[10,1,4,256]{3,1,2,0:T(2,128)(2,1)S(1)}, u32[]{:S(2)}, u32[]{:S(2)}) collective-permute-start(bf16[10,1,4,256]{3,1,2,0:T(2,128)(2,1)S(1)} %get-tuple-element.51), channel_id=1, source_target_pairs={{1,0},{2,1},{3,2},{4,3},{5,4},{6,5},{7,6},{8,7},{9,8},{10,9},{11,1... | collective-permute-start | bytes 61448 | tf_op jit(solution)/shard_map/ppermute | solution.py:18
  107.0 1.6 copy.158
  109.5 1.6 copy.157
  112.7 1.6 copy.155
  115.9 1.7 fusion.105
  117.7 1.8 fusion.29
  144.0 1.6 copy.163
  153.2 1.6 reshape.400
  155.6 1.7 reshape.407
  158.0 1.6 reshape.405
  160.3 1.6 reshape.404
  161.9 1.6 copy.176
  163.6 1.6 reshape.402
  165.2 1.6 copy.175
  166.8 1.6 reshape.401
  168.4 1.6 copy.173
  178.9 1.6 reshape.393
  182.9 1.6 reshape.390
  185.9 1.7 reshape.387
  192.1 118.8 %all-reduce.5.cloned.1.call-done = f32[6912,128]{1,0:T(8,128)} async-done(((f32[6912,128]{1,0:T(8,128)}), f32[6912,128]{1,0:T(8,128)}) %all-reduce.5.cloned.1.call-update) | async-done | bytes 3538960 | tf_op jit(solution)/shard_map/psum | solution.py:104
  314.1 76.8 %all-reduce.7.cloned.1.call-done = f32[6912,128]{1,0:T(8,128)} async-done(((f32[6912,128]{1,0:T(8,128)}), f32[6912,128]{1,0:T(8,128)}) %all-reduce.7.cloned.1.call-update) | async-done | bytes 3538960 | tf_op jit(solution)/shard_map/psum | solution.py:104
  390.9 3.4 multiply_convert_fusion
  (261 shorter events, 90.5 us)
Async XLA Ops:
  9.6 27.5 %all-to-all-start.1 = ((s32[64,1,1]{2,1,0:T(1,128)}), s32[64,1,1]{2,1,0:T(1,128)S(1)}, u32[]{:S(2)}, u32[]{:S(2)}) async-start(s32[64,1,1]{2,1,0:T(1,128)} %copy.183), calls=%async_computation.1 | async-start | bytes 65536 | tf_op jit(solution)/shard_map/all_to_all | solution.py:48
  37.2 30.0 %all-to-all-start = ((bf16[64,4,256]{2,1,0:T(4,128)(2,1)}), bf16[64,4,256]{2,1,0:T(4,128)(2,1)S(1)}, u32[]{:S(2)}, u32[]{:S(2)}) async-start(bf16[64,4,256]{2,1,0:T(4,128)(2,1)} %reshape.379), calls=%async_computation | async-start | bytes 262144 | tf_op jit(solution)/shard_map/all_to_all | solution.py:41
  42.7 19.1 %copy-start = (bf16[27,256,128]{2,1,0:T(8,128)(2,1)S(1)}, bf16[27,256,128]{2,1,0:T(8,128)(2,1)}, u32[]{:S(2)}) copy-start(bf16[27,256,128]{2,1,0:T(8,128)(2,1)} %param.8) | copy-start | bytes 5308420
  46.6 5.3 %collective-permute-start.5 = (bf16[1,8,4,128]{3,2,1,0:T(4,128)(2,1)S(1)}, bf16[1,8,4,128]{3,2,1,0:T(4,128)(2,1)S(1)}, u32[]{:S(2)}, u32[]{:S(2)}) collective-permute-start(bf16[1,8,4,128]{3,2,1,0:T(4,128)(2,1)S(1)} %bitcast.495), channel_id=1, source_target_pairs={{64,0},{128,64},{192,128},{256,192},{320,256},{384,320},{448,384},... | collective-permute-start | bytes 24584 | tf_op jit(solution)/shard_map/ppermute | solution.py:18
  47.9 4.0 %collective-permute-start.4 = (bf16[1,8,4,128]{3,2,1,0:T(4,128)(2,1)S(1)}, bf16[1,8,4,128]{3,2,1,0:T(4,128)(2,1)S(1)}, u32[]{:S(2)}, u32[]{:S(2)}) collective-permute-start(bf16[1,8,4,128]{3,2,1,0:T(4,128)(2,1)S(1)} %bitcast.494), channel_id=1, source_target_pairs={{0,64},{64,128},{128,192},{192,256},{256,320},{320,384},{384,448},... | collective-permute-start | bytes 24584 | tf_op jit(solution)/shard_map/ppermute | solution.py:16
  51.9 8.0 %collective-permute-start.6 = (bf16[10,1,4,128]{3,2,1,0:T(4,128)(2,1)S(1)}, bf16[10,1,4,128]{3,2,1,0:T(4,128)(2,1)S(1)}, u32[]{:S(2)}, u32[]{:S(2)}) collective-permute-start(bf16[10,1,4,128]{3,2,1,0:T(4,128)(2,1)S(1)} %get-tuple-element.65), channel_id=1, source_target_pairs={{0,1},{1,2},{2,3},{3,4},{4,5},{5,6},{6,7},{7,8},{8,9},{9,10},{10,1... | collective-permute-start | bytes 30728 | tf_op jit(solution)/shard_map/ppermute | solution.py:16
  55.3 5.9 %collective-permute-start.7 = (bf16[10,1,4,128]{3,2,1,0:T(4,128)(2,1)S(1)}, bf16[10,1,4,128]{3,2,1,0:T(4,128)(2,1)S(1)}, u32[]{:S(2)}, u32[]{:S(2)}) collective-permute-start(bf16[10,1,4,128]{3,2,1,0:T(4,128)(2,1)S(1)} %get-tuple-element.66), channel_id=1, source_target_pairs={{1,0},{2,1},{3,2},{4,3},{5,4},{6,5},{7,6},{8,7},{9,8},{10,9},{11,1... | collective-permute-start | bytes 30728 | tf_op jit(solution)/shard_map/ppermute | solution.py:18
  68.7 17.8 %collective-permute-start = (bf16[1,8,4,256]{3,1,2,0:T(8,128)(2,1)S(1)}, bf16[1,8,4,256]{3,1,2,0:T(8,128)(2,1)S(1)}, u32[]{:S(2)}, u32[]{:S(2)}) collective-permute-start(bf16[1,8,4,256]{3,1,2,0:T(8,128)(2,1)S(1)} %copy.152), channel_id=1, source_target_pairs={{0,64},{64,128},{128,192},{192,256},{256,320},{320,384},{384,448},... | collective-permute-start | bytes 49160 | tf_op jit(solution)/shard_map/ppermute | solution.py:16
  72.6 26.5 %all-to-all-start.2 = ((bf16[64,4,256]{2,1,0:T(4,128)(2,1)}), bf16[64,4,256]{2,1,0:T(4,128)(2,1)S(1)}, u32[]{:S(2)}, u32[]{:S(2)}) async-start(bf16[64,4,256]{2,1,0:T(4,128)(2,1)} %reshape.436), calls=%async_computation.2 | async-start | bytes 262144 | tf_op jit(solution)/shard_map/all_to_all | solution.py:108
  85.0 225.9 %all-reduce.5.cloned.1.call-start = ((), (), s32[]{:S(2)}) async-start(), calls=%async_computation.3 | async-start | bytes 7077888 | tf_op jit(solution)/shard_map/psum | solution.py:104
  85.1 13.8 %copy-start.24 = (bf16[8,8,4,256]{3,2,1,0:T(4,128)(2,1)}, bf16[8,8,4,256]{3,2,1,0:T(4,128)(2,1)S(1)}, u32[]{:S(2)}) copy-start(bf16[8,8,4,256]{3,2,1,0:T(4,128)(2,1)S(1)} %reshape.381) | copy-start | bytes 393220
  85.2 5.5 %collective-permute-start.1 = (bf16[1,8,4,256]{3,1,2,0:T(8,128)(2,1)S(1)}, bf16[1,8,4,256]{3,1,2,0:T(8,128)(2,1)S(1)}, u32[]{:S(2)}, u32[]{:S(2)}) collective-permute-start(bf16[1,8,4,256]{3,1,2,0:T(8,128)(2,1)S(1)} %copy.153), channel_id=1, source_target_pairs={{64,0},{128,64},{192,128},{256,192},{320,256},{384,320},{448,384},... | collective-permute-start | bytes 49160 | tf_op jit(solution)/shard_map/ppermute | solution.py:18
  86.5 14.1 %copy-start.41 = (bf16[9,8,4,256]{3,1,2,0:T(8,128)(2,1)}, bf16[9,8,4,256]{3,1,2,0:T(8,128)(2,1)S(1)}, u32[]{:S(2)}) copy-start(bf16[9,8,4,256]{3,1,2,0:T(8,128)(2,1)S(1)} %get-tuple-element.53) | copy-start | bytes 442372
  90.7 10.0 %copy-start.35 = (bf16[9,8,4,256]{3,1,2,0:T(8,128)(2,1)}, bf16[9,8,4,256]{3,1,2,0:T(8,128)(2,1)S(1)}, u32[]{:S(2)}) copy-start(bf16[9,8,4,256]{3,1,2,0:T(8,128)(2,1)S(1)} %get-tuple-element.71) | copy-start | bytes 442372
  90.7 9.9 %collective-permute-start.2 = (bf16[10,1,4,256]{3,1,2,0:T(2,128)(2,1)S(1)}, bf16[10,1,4,256]{3,1,2,0:T(2,128)(2,1)S(1)}, u32[]{:S(2)}, u32[]{:S(2)}) collective-permute-start(bf16[10,1,4,256]{3,1,2,0:T(2,128)(2,1)S(1)} %get-tuple-element.50), channel_id=1, source_target_pairs={{0,1},{1,2},{2,3},{3,4},{4,5},{5,6},{6,7},{7,8},{8,9},{9,10},{10,1... | collective-permute-start | bytes 61448 | tf_op jit(solution)/shard_map/ppermute | solution.py:16
  94.1 6.6 %collective-permute-start.3 = (bf16[10,1,4,256]{3,1,2,0:T(2,128)(2,1)S(1)}, bf16[10,1,4,256]{3,1,2,0:T(2,128)(2,1)S(1)}, u32[]{:S(2)}, u32[]{:S(2)}) collective-permute-start(bf16[10,1,4,256]{3,1,2,0:T(2,128)(2,1)S(1)} %get-tuple-element.51), channel_id=1, source_target_pairs={{1,0},{2,1},{3,2},{4,3},{5,4},{6,5},{7,6},{8,7},{9,8},{10,9},{11,1... | collective-permute-start | bytes 61448 | tf_op jit(solution)/shard_map/ppermute | solution.py:18
  122.1 1.8 copy-start.32
  141.6 249.3 %all-reduce.7.cloned.1.call-start = ((), (), s32[]{:S(2)}) async-start(), calls=%async_computation.4 | async-start | bytes 7077888 | tf_op jit(solution)/shard_map/psum | solution.py:104
  142.5 3.2 copy-start.31
  142.5 3.9 copy-start.29
  142.5 4.6 %copy-start.27 = (bf16[8,8,4,256]{3,1,2,0:T(8,128)(2,1)S(1)}, bf16[8,8,4,256]{3,1,2,0:T(8,128)(2,1)}, u32[]{:S(2)}) copy-start(bf16[8,8,4,256]{3,1,2,0:T(8,128)(2,1)} %get-tuple-element.49) | copy-start | bytes 393220
  142.7 12.2 %copy-start.8 = (bf16[8,8,4,256]{3,1,2,0:T(8,128)(2,1)S(1)}, bf16[8,8,4,256]{3,1,2,0:T(8,128)(2,1)}, u32[]{:S(2)}) copy-start(bf16[8,8,4,256]{3,1,2,0:T(8,128)(2,1)} %get-tuple-element.5) | copy-start | bytes 393220
  142.9 14.4 %copy-start.7 = (bf16[8,8,4,256]{3,1,2,0:T(8,128)(2,1)S(1)}, bf16[8,8,4,256]{3,1,2,0:T(8,128)(2,1)}, u32[]{:S(2)}) copy-start(bf16[8,8,4,256]{3,1,2,0:T(8,128)(2,1)} %get-tuple-element.6) | copy-start | bytes 393220
  144.0 15.6 %copy-start.5 = (bf16[8,8,4,256]{3,1,2,0:T(8,128)(2,1)S(1)}, bf16[8,8,4,256]{3,1,2,0:T(8,128)(2,1)}, u32[]{:S(2)}) copy-start(bf16[8,8,4,256]{3,1,2,0:T(8,128)(2,1)} %get-tuple-element.7) | copy-start | bytes 393220
  153.2 18.3 %copy-start.4 = (bf16[8,8,4,256]{3,1,2,0:T(8,128)(2,1)S(1)}, bf16[8,8,4,256]{3,1,2,0:T(8,128)(2,1)}, u32[]{:S(2)}) copy-start(bf16[8,8,4,256]{3,1,2,0:T(8,128)(2,1)} %get-tuple-element.11) | copy-start | bytes 393220
  155.6 17.6 %copy-start.3 = (bf16[8,8,4,256]{3,1,2,0:T(8,128)(2,1)S(1)}, bf16[8,8,4,256]{3,1,2,0:T(8,128)(2,1)}, u32[]{:S(2)}) copy-start(bf16[8,8,4,256]{3,1,2,0:T(8,128)(2,1)} %get-tuple-element.12) | copy-start | bytes 393220
  158.0 16.9 %copy-start.2 = (bf16[8,8,4,256]{3,1,2,0:T(8,128)(2,1)S(1)}, bf16[8,8,4,256]{3,1,2,0:T(8,128)(2,1)}, u32[]{:S(2)}) copy-start(bf16[8,8,4,256]{3,1,2,0:T(8,128)(2,1)} %get-tuple-element.13) | copy-start | bytes 393220
  160.3 16.2 %copy-start.1 = (bf16[8,8,4,256]{3,1,2,0:T(8,128)(2,1)S(1)}, bf16[8,8,4,256]{3,1,2,0:T(8,128)(2,1)}, u32[]{:S(2)}) copy-start(bf16[8,8,4,256]{3,1,2,0:T(8,128)(2,1)} %get-tuple-element.14) | copy-start | bytes 393220
  180.5 9.4 %copy-start.20 = (bf16[256,256]{1,0:T(8,128)(2,1)S(1)}, bf16[256,256]{1,0:T(8,128)(2,1)}, u32[]{:S(2)}) copy-start(bf16[256,256]{1,0:T(8,128)(2,1)} %reshape.389) | copy-start | bytes 393220
  184.5 6.0 %copy-start.17 = (bf16[256,256]{1,0:T(8,128)(2,1)S(1)}, bf16[256,256]{1,0:T(8,128)(2,1)}, u32[]{:S(2)}) copy-start(bf16[256,256]{1,0:T(8,128)(2,1)} %reshape.392) | copy-start | bytes 393220
  185.9 4.8 %copy-start.22 = (bf16[256,256]{1,0:T(8,128)(2,1)S(1)}, bf16[256,256]{1,0:T(8,128)(2,1)}, u32[]{:S(2)}) copy-start(bf16[256,256]{1,0:T(8,128)(2,1)} %reshape.393) | copy-start | bytes 393220
  187.6 2.5 copy-start.23
  (24 other events, 30.0 us)
Sparse Core Ops, SparseCore 0:
  141.7 169.1 all-reduce.4
  313.4 77.4 all-reduce.6
